TPU v7x, 32 devices: a whole 2x2x4 slice. The times are simulated.
32 devices in a mesh: dp: 8 (over z, y), tensor: 4 (over x, core).
Axes of the slice: x: 2, y: 2, z: 4, core: 2. Of those that a mesh axis runs over, the one named last changes fastest.
Arguments:
- tokens: bfloat16 [32768, 768], P(('dp', 'tensor')), may hold values from -6 to 6
- segment_ids: int32 [16, 2048], P('dp'), may hold values from 0 to 15, never falling along the last dimension, each value on 1 to 1024 neighbouring positions
- qkv_weight: bfloat16 [768, 3, 768], P('dp', None, 'tensor'), may hold values from -0.21875 to 0.21875
- qv_bias: bfloat16 [2, 768], P(None, 'tensor'), may hold values from -2 to 2
- out_weight: bfloat16 [768, 768], P('dp', 'tensor'), may hold values from -0.4375 to 0.4375
- out_bias: bfloat16 [768], replicated, may hold values from -2 to 2
- first_gain: bfloat16 [768], replicated, may hold values from 0.25 to 1.75
- first_shift: bfloat16 [768], replicated, may hold values from -2 to 2
- up_weight: bfloat16 [768, 3072], P('dp', 'tensor'), may hold values from -0.21875 to 0.21875
- up_bias: bfloat16 [3072], P('tensor'), may hold values from -3 to 3
- down_weight: bfloat16 [768, 3072], P('dp', 'tensor'), may hold values from -0.109375 to 0.109375
- down_bias: bfloat16 [768], replicated, may hold values from -2 to 2
- second_gain: bfloat16 [768], replicated, may hold values from 0.25 to 1.75
- second_shift: bfloat16 [768], replicated, may hold values from -2 to 2
- output_grad: bfloat16 [32768, 768], P(('dp', 'tensor')), may hold values from -6 to 6
Outputs:
- output: bfloat16 [32768, 768], P(('dp', 'tensor'))
- input_grad: float32 [32768, 768], P(('dp', 'tensor'))
- qkv_grad: float32 [768, 3, 768], P('dp', None, 'tensor')
- qv_bias_grad: float32 [2, 768], P(None, 'tensor')
- out_weight_grad: float32 [768, 768], P('dp', 'tensor')
- up_weight_grad: float32 [768, 3072], P('dp', 'tensor')
- up_bias_grad: float32 [3072], P('tensor')
- down_weight_grad: float32 [768, 3072], P('dp', 'tensor')
- vector_grads: float32 [6, 768], replicated
Inputs may be any that keep to these rules, and one draw needn't show every extreme that they name: `segment_ids`: document ids never fall along a sequence; each document has at most 1024 tokens.
All inputs are finite; a program needn't handle non-finite values.
Results may differ from a plain program's by a relative error of at most 0.015.
Values may be sent and summed in bfloat16 or wider, within the bound.
No kernel may reach another device: no remote copies, remote signals or barrier semaphores. Data moves between devices by JAX's collectives and lax.ppermute only.
A program may use at most 192 MiB of HBM per device.

v0:
```python
from functools import partial
import jax
import jax.numpy as jnp
from jax import lax
from jax.sharding import PartitionSpec as P

HEAD_DIM = 64
EPSILON = 1e-12
MASKED = -1e30


def matmul_plain(left, right):
    return jnp.dot(left, right, preferred_element_type=jnp.float32)


def times_transposed(left, right):
    return lax.dot_general(
        left, right, (((1,), (1,)), ((), ())), preferred_element_type=jnp.float32
    )


def over_rows(left, right):
    return lax.dot_general(
        left, right, (((0,), (0,)), ((), ())), preferred_element_type=jnp.float32
    )


def normalize(values, gain, shift):
    center = jnp.mean(values, axis=-1, keepdims=True)
    offset = values - center
    spread = jnp.mean(offset * offset, axis=-1, keepdims=True)
    inverse = lax.rsqrt(spread + EPSILON)
    normed = offset * inverse
    return (normed * gain + shift, normed, inverse)


def normalize_back(incoming, normed, inverse, gain):
    weighted = incoming * gain
    centered = weighted - jnp.mean(weighted, axis=-1, keepdims=True)
    centered = centered - normed * jnp.mean(weighted * normed, axis=-1, keepdims=True)
    return (centered * inverse, jnp.sum(incoming * normed, axis=0), jnp.sum(incoming, axis=0))


def masked_scores(query_rows, seg_rows, key_seq, seg_seq):
    scores = jnp.einsum(
        "qhd,khd->hqk", query_rows, key_seq, preferred_element_type=jnp.float32
    ) * HEAD_DIM ** (-0.5)
    same_doc = (seg_rows[:, None] == seg_seq[None, :])[None]
    return jnp.where(same_doc, scores, MASKED)


def attend_forward(query_seq, key_seq, value_seq, seg_seq, block_rows):
    block_count = query_seq.shape[0] // block_rows

    def one_block(block_index):
        first_row = block_index * block_rows
        query_rows = lax.dynamic_slice_in_dim(query_seq, first_row, block_rows, 0)
        seg_rows = lax.dynamic_slice_in_dim(seg_seq, first_row, block_rows, 0)
        scores = masked_scores(query_rows, seg_rows, key_seq, seg_seq)
        row_max = jnp.max(scores, axis=-1, keepdims=True)
        powers = jnp.exp(scores - row_max)
        row_total = jnp.sum(powers, axis=-1, keepdims=True)
        weights = (powers / row_total).astype(jnp.bfloat16)
        context = jnp.einsum("hqk,khd->qhd", weights, value_seq, preferred_element_type=jnp.float32)
        return (context, (row_max + jnp.log(row_total))[..., 0])

    contexts, log_sums = lax.map(one_block, jnp.arange(block_count, dtype=jnp.int32))
    return (contexts.reshape(query_seq.shape), log_sums)


def attend_backward(query_seq, key_seq, value_seq, seg_seq, log_sums, grad_seq, block_rows):
    block_count = query_seq.shape[0] // block_rows
    score_scale = HEAD_DIM ** (-0.5)

    def one_block(running, block_index):
        key_grad, value_grad = running
        first_row = block_index * block_rows
        query_rows = lax.dynamic_slice_in_dim(query_seq, first_row, block_rows, 0)
        seg_rows = lax.dynamic_slice_in_dim(seg_seq, first_row, block_rows, 0)
        grad_rows = lax.dynamic_slice_in_dim(grad_seq, first_row, block_rows, 0)
        scores = masked_scores(query_rows, seg_rows, key_seq, seg_seq)
        probs = jnp.exp(scores - log_sums[block_index][..., None])
        weights = probs.astype(jnp.bfloat16)
        prob_grad = jnp.einsum(
            "qhd,khd->hqk", grad_rows, value_seq, preferred_element_type=jnp.float32
        )
        inner = jnp.sum(probs * prob_grad, axis=-1, keepdims=True)
        score_grad = (probs * (prob_grad - inner)).astype(jnp.bfloat16)
        query_grad = (
            jnp.einsum("hqk,khd->qhd", score_grad, key_seq, preferred_element_type=jnp.float32)
            * score_scale
        )
        key_grad = (
            key_grad
            + jnp.einsum("hqk,qhd->khd", score_grad, query_rows, preferred_element_type=jnp.float32)
            * score_scale
        )
        value_grad = value_grad + jnp.einsum(
            "hqk,qhd->khd", weights, grad_rows, preferred_element_type=jnp.float32
        )
        return ((key_grad, value_grad), query_grad)

    empty_grad = jnp.zeros(key_seq.shape, jnp.float32)
    (key_grad, value_grad), query_grads = lax.scan(
        one_block, (empty_grad, empty_grad), jnp.arange(block_count, dtype=jnp.int32)
    )
    return (query_grads.reshape(query_seq.shape), key_grad, value_grad)


def local(
    tokens,
    segment_ids,
    qkv_weight,
    qv_bias,
    out_weight,
    out_bias,
    first_gain,
    first_shift,
    up_weight,
    up_bias,
    down_weight,
    down_bias,
    second_gain,
    second_shift,
    output_grad,
):
    row_count, model_width = tokens.shape
    sequences, seq_length = segment_ids.shape
    block_rows = min(512, seq_length)
    gathered = lax.all_gather(tokens, "tensor", axis=0, tiled=True)
    qkv_full, out_full, up_full, down_full = (
        lax.all_gather(qkv_weight, "dp", axis=0, tiled=True),
        lax.all_gather(out_weight, "dp", axis=0, tiled=True),
        lax.all_gather(up_weight, "dp", axis=0, tiled=True),
        lax.all_gather(down_weight, "dp", axis=0, tiled=True),
    )
    local_width = qkv_full.shape[2]
    shape_four = (sequences, seq_length, local_width // HEAD_DIM, HEAD_DIM)
    qkv_flat = qkv_full.reshape(model_width, 3 * local_width)
    bias_pair = qv_bias.astype(jnp.float32)
    projected = matmul_plain(gathered, qkv_flat)
    queries = (projected[:, :local_width] + bias_pair[0]).astype(jnp.bfloat16).reshape(shape_four)
    keys_all = projected[:, local_width : 2 * local_width].astype(jnp.bfloat16).reshape(shape_four)
    values_all = (
        (projected[:, 2 * local_width :] + bias_pair[1]).astype(jnp.bfloat16).reshape(shape_four)
    )

    def forward_sequence(packed):
        return attend_forward(packed[0], packed[1], packed[2], packed[3], block_rows)

    contexts, log_sums = lax.map(forward_sequence, (queries, keys_all, values_all, segment_ids))
    context = contexts.reshape(-1, local_width).astype(jnp.bfloat16)
    attended = lax.psum_scatter(
        times_transposed(context, out_full), "tensor", scatter_dimension=0, tiled=True
    )
    gain_one = first_gain.astype(jnp.float32)
    gain_two = second_gain.astype(jnp.float32)
    first, normed_one, inverse_one = normalize(
        tokens.astype(jnp.float32) + attended + out_bias.astype(jnp.float32),
        gain_one,
        first_shift.astype(jnp.float32),
    )
    first_low = first.astype(jnp.bfloat16)
    spread_rows = lax.all_gather(first_low, "tensor", axis=0, tiled=True)
    up_used, down_used = (up_full, down_full)
    hidden_bias = up_bias.astype(jnp.float32)
    hidden_pre = matmul_plain(spread_rows, up_used) + hidden_bias
    activated, gelu_back = jax.vjp(partial(jax.nn.gelu, approximate=False), hidden_pre)
    act_low = activated.astype(jnp.bfloat16)
    fed = lax.psum_scatter(
        times_transposed(
            lax.slice_in_dim(act_low, 0, lax.axis_size("tensor") * row_count, axis=0), down_used
        ).astype(jnp.bfloat16),
        "tensor",
        scatter_dimension=0,
        tiled=True,
    ).astype(jnp.float32)
    second, normed_two, inverse_two = normalize(
        first + fed + down_bias.astype(jnp.float32), gain_two, second_shift.astype(jnp.float32)
    )
    output = second.astype(jnp.bfloat16)
    grad_second, gain_two_g, shift_two_g = normalize_back(
        output_grad.astype(jnp.float32), normed_two, inverse_two, gain_two
    )
    fed_low = grad_second.astype(jnp.bfloat16)
    down_bias_g = jnp.sum(fed_low.astype(jnp.float32), axis=0)
    fed_rows = lax.all_gather(fed_low, "tensor", axis=0, tiled=True)
    act_grad = matmul_plain(fed_rows, down_used)
    pre_grad = gelu_back(act_grad)[0].astype(jnp.bfloat16)
    down_grad = over_rows(fed_rows, act_low)
    up_grad = over_rows(spread_rows, pre_grad)
    up_bias_g = jnp.sum(pre_grad.astype(jnp.float32), axis=0)
    first_grad = lax.psum_scatter(
        times_transposed(pre_grad, up_used).astype(jnp.bfloat16),
        "tensor",
        scatter_dimension=0,
        tiled=True,
    ).astype(jnp.float32)
    grad_first, gain_one_g, shift_one_g = normalize_back(
        grad_second + first_grad, normed_one, inverse_one, gain_one
    )
    attn_low = grad_first.astype(jnp.bfloat16)
    out_bias_g = jnp.sum(attn_low.astype(jnp.float32), axis=0)
    attn_rows = lax.all_gather(attn_low, "tensor", axis=0, tiled=True)
    context_grad = matmul_plain(attn_rows, out_full).astype(jnp.bfloat16).reshape(shape_four)
    out_weight_g = over_rows(attn_rows, context)

    def backward_sequence(packed):
        return attend_backward(
            packed[0], packed[1], packed[2], packed[3], packed[4], packed[5], block_rows
        )

    query_g, key_g, value_g = lax.map(
        backward_sequence, (queries, keys_all, values_all, segment_ids, log_sums, context_grad)
    )
    mixed_grad = jnp.concatenate(
        [
            query_g.reshape(-1, local_width),
            key_g.reshape(-1, local_width),
            value_g.reshape(-1, local_width),
        ],
        axis=1,
    ).astype(jnp.bfloat16)
    qkv_g = over_rows(gathered, mixed_grad).reshape(model_width, 3, local_width)
    mixed_wide = mixed_grad.astype(jnp.float32)
    qv_g = jnp.stack(
        [
            jnp.sum(mixed_wide[:, :local_width], axis=0),
            jnp.sum(mixed_wide[:, 2 * local_width :], axis=0),
        ]
    )
    input_grad = grad_first + lax.psum_scatter(
        times_transposed(mixed_grad, qkv_flat).astype(jnp.bfloat16),
        "tensor",
        scatter_dimension=0,
        tiled=True,
    ).astype(jnp.float32)
    qkv_share, out_share, up_share, down_share = (
        lax.psum_scatter(qkv_g, "dp", scatter_dimension=0, tiled=True),
        lax.psum_scatter(out_weight_g, "dp", scatter_dimension=0, tiled=True),
        lax.psum_scatter(up_grad, "dp", scatter_dimension=0, tiled=True),
        lax.psum_scatter(down_grad, "dp", scatter_dimension=0, tiled=True),
    )
    qv_share, up_bias_share = lax.psum((qv_g, up_bias_g), "dp")
    vectors = lax.psum(
        jnp.stack([out_bias_g, gain_one_g, shift_one_g, down_bias_g, gain_two_g, shift_two_g]),
        ("dp", "tensor"),
    )
    return (
        output,
        input_grad,
        qkv_share,
        qv_share,
        out_share,
        up_share,
        up_bias_share,
        down_share,
        vectors,
    )


def solution(mesh):
    in_specs = (
        P(("dp", "tensor"), None),
        P("dp", None),
        P("dp", None, "tensor"),
        P(None, "tensor"),
        P("dp", "tensor"),
        P(),
        P(),
        P(),
        P("dp", "tensor"),
        P("tensor"),
        P("dp", "tensor"),
        P(),
        P(),
        P(),
        P(("dp", "tensor"), None),
    )
    out_specs = (
        P(("dp", "tensor"), None),
        P(("dp", "tensor"), None),
        P("dp", None, "tensor"),
        P(None, "tensor"),
        P("dp", "tensor"),
        P("dp", "tensor"),
        P("tensor"),
        P("dp", "tensor"),
        P(),
    )
    return jax.shard_map(local, mesh=mesh, in_specs=in_specs, out_specs=out_specs, check_vma=False)
```

profile of v0, /device:TPU:0, one launch (start us, length us, event | category | flops | bytes accessed | tf_op | source)
XLA Modules:
  0.0 1469.7 jit_solution(13262983610031420961)
XLA Ops:
  9.9 38.8 %all_gather.25 = bf16[768,3,192]{2,1,0:T(4,128)(2,1)S(1)} all-gather(bf16[96,3,192]{2,1,0:T(4,128)(2,1)S(1)} %copy.55), channel_id=1, replica_groups=mesh['dp'=8,'tensor'=4] {'dp'}, dimensions={0}, use_global_device_ids=true | all-gather | bytes 995328 | tf_op jit(solution)/shard_map/all_gather | solution.py:132
  49.6 33.1 %all_gather.26 = bf16[768,192]{1,0:T(8,128)(2,1)} all-gather(bf16[96,192]{1,0:T(8,128)(2,1)S(1)} %copy-done.24), channel_id=1, replica_groups=mesh['dp'=8,'tensor'=4] {'dp'}, dimensions={0}, use_global_device_ids=true | all-gather | bytes 331776 | tf_op jit(solution)/shard_map/all_gather | solution.py:133
  109.5 194.5 %while.54 = (s32[]{:T(128)}, bf16[2,2048,3,64]{3,2,1,0:T(4,128)(2,1)}, f32[2,4,3,512]{3,2,1,0:T(4,128)S(1)}, bf16[2,2048,3,64]{1,3,2,0:T(8,128)(2,1)}, s32[2,204...) while((s32[]{:T(128)}, ...), condition=%wide.region_5.6_spmd, body=%wide.region_0.5_spmd.sunk | while | flops 844102144 | bytes 53436884 | solution.py:151
  113.1 90.5 %while.57 = (s32[]{:T(128)}, bf16[4,512,3,64]{1,3,2,0:T(8,128)(2,1)S(1)}, f32[4,3,512]{2,1,0:T(4,128)S(1)}, s32[4]{0:T(128)S(1)}, s32[2048]{0:T(1024)S(1)}, /*in...) while((s32[]{:T(128)}, ...), condition=%wide.region_4.4_spmd, body=%wide.region_1.3_spmd.sunk | while | flops 844102144 | bytes 44179652 | solution.py:67
  115.1 7.1 fusion.128
  122.2 6.8 fusion.129
  129.0 6.7 fusion.130
  137.7 7.1 fusion.128
  144.8 6.8 fusion.129
  151.6 6.7 fusion.130
  160.3 7.1 fusion.128
  167.5 6.8 fusion.129
  174.2 6.7 fusion.130
  182.9 7.1 fusion.128
  190.1 6.8 fusion.129
  196.8 6.7 fusion.130
  210.4 90.5 %while.57 = (s32[]{:T(128)}, bf16[4,512,3,64]{1,3,2,0:T(8,128)(2,1)S(1)}, f32[4,3,512]{2,1,0:T(4,128)S(1)}, s32[4]{0:T(128)S(1)}, s32[2048]{0:T(1024)S(1)}, /*in...) while((s32[]{:T(128)}, ...), condition=%wide.region_4.4_spmd, body=%wide.region_1.3_spmd.sunk | while | flops 844102144 | bytes 44179652 | solution.py:67
  212.3 7.1 fusion.128
  219.5 6.8 fusion.129
  226.2 6.7 fusion.130
  235.0 7.1 fusion.128
  242.1 6.8 fusion.129
  248.9 6.7 fusion.130
  257.6 7.1 fusion.128
  264.7 6.8 fusion.129
  271.5 6.7 fusion.130
  280.2 7.1 fusion.128
  287.4 6.8 fusion.129
  294.1 6.7 fusion.130
  304.0 9.9 copy.60
  315.8 6.4 fusion.59
  322.9 97.6 %reduce-scatter.9.cloned.1.call-done = f32[1024,768]{1,0:T(8,128)} async-done(((f32[4096,768]{1,0:T(8,128)}), f32[1024,768]{1,0:T(8,128)}) %reduce-scatter.9.cloned.1.call-update) | async-done | bytes 3145744 | tf_op jit(solution)/shard_map/reduce_scatter | solution.py:153
  426.3 45.7 %all-gather.9.cloned.1.call-done = bf16[4096,768]{1,0:T(8,128)(2,1)} async-done(((bf16[1024,768]{1,0:T(8,128)(2,1)}), bf16[4096,768]{1,0:T(8,128)(2,1)}) %all-gather.9.cloned.1.call-update) | async-done | bytes 6291472 | tf_op jit(solution)/shard_map/all_gather | solution.py:164
  471.9 34.8 %multiply_convert_fusion.1 = (bf16[4096,768]{1,0:T(8,128)(2,1)}, f32[4096,768]{1,0:T(8,128)}, f32[4096,768]{1,0:T(8,128)}) fusion(f32[768]{0:T(1024)S(1)} %convert_element_type.114, bf16[4096,768]{1,0:T(8,128)(2,1)} %all-gather.9.cloned.1.call-done, bf16[768,768]{1,0:T(8,128)(2,1)} %all-gather.11.cloned.1.call-done), kind=kOutput, calls=%fused_computation.62 | convolution fusion | flops 5039456256 | bytes 38931456 | tf_op jit(solution)/shard_map/dot_general | solution.py:13
  506.8 8.8 all-gather.13.cloned.1.call-done
  515.5 9.1 convolution_convert_fusion.2
  525.4 56.1 %reduce-scatter.11.cloned.1.call-done = bf16[1024,768]{1,0:T(8,128)(2,1)} async-done(((bf16[4096,768]{1,0:T(8,128)(2,1)}), bf16[1024,768]{1,0:T(8,128)(2,1)}) %reduce-scatter.11.cloned.1.call-update) | async-done | bytes 1572880 | tf_op jit(solution)/shard_map/reduce_scatter | solution.py:170
  591.3 46.3 %all-gather.15.cloned.1.call-done = bf16[4096,768]{1,0:T(8,128)(2,1)} async-done(((bf16[1024,768]{1,0:T(8,128)(2,1)}), bf16[4096,768]{1,0:T(8,128)(2,1)}) %all-gather.15.cloned.1.call-update) | async-done | bytes 6291472 | tf_op jit(solution)/shard_map/all_gather | solution.py:187
  637.6 19.0 %convert_reduce_fusion = (f32[768]{0:T(1024)}, bf16[4096,768]{1,0:T(8,128)(2,1)}) fusion(f32[4096,768]{1,0:T(8,128)} %get-tuple-element.390, f32[4096,768]{1,0:T(8,128)} %get-tuple-element.406, f32[768]{0:T(1024)S(1)} %convert_element_type.114, bf16[4096,768]{1,0:T(8,128)(2,1)} %all-gather.15.cloned.1.call-done, ...), kind=kOutput, calls=%fused_computation.60 | convolution fusion | flops 4885314560 | bytes 38934528 | tf_op jit(solution)/shard_map/dot_general | solution.py:13
  656.6 9.7 convolution_convert_fusion.1
  666.4 58.5 %reduce-scatter.13.cloned.1.call-done = bf16[1024,768]{1,0:T(8,128)(2,1)} async-done(((bf16[4096,768]{1,0:T(8,128)(2,1)}), bf16[1024,768]{1,0:T(8,128)(2,1)}) %reduce-scatter.13.cloned.1.call-update) | async-done | bytes 1572880 | tf_op jit(solution)/shard_map/reduce_scatter | solution.py:193
  732.6 46.3 %all-gather.17.cloned.1.call-done = bf16[4096,768]{1,0:T(8,128)(2,1)} async-done(((bf16[1024,768]{1,0:T(8,128)(2,1)}), bf16[4096,768]{1,0:T(8,128)(2,1)}) %all-gather.17.cloned.1.call-update) | async-done | bytes 6291472 | tf_op jit(solution)/shard_map/all_gather | solution.py:204
  789.7 301.7 %while.56 = (s32[]{:T(128)}, bf16[2,2048,3,64]{3,2,1,0:T(4,128)(2,1)}, bf16[2,2048,3,64]{1,3,2,0:T(8,128)(2,1)}, bf16[2,2048,3,64]{1,3,2,0:T(8,128)(2,1)}, bf16[...) while((s32[]{:T(128)}, ...), condition=%wide.region_21.22_spmd, body=%wide.region_17.21_spmd.sunk | while | flops 2063563264 | bytes 193981360 | solution.py:213
  797.1 132.6 %while.58 = (s32[]{:T(128)}, f32[2048,3,64]{0,2,1:T(8,128)}, f32[2048,3,64]{0,2,1:T(8,128)}, bf16[4,512,3,64]{1,3,2,0:T(8,128)(2,1)}, s32[4]{0:T(128)S(1)}, /*in...) while((s32[]{:T(128)}, f32[2048,3,64]{0,2,1:T(8,128)}, ...), condition=%wide.region_20.20_spmd.clone, body=%wide.region_18.19_spmd.clone.sunk | while | flops 2063563264 | bytes 156690960 | solution.py:104
  813.6 6.2 multiply_convert_fusion.3
  846.0 6.2 multiply_convert_fusion.3
  879.8 6.2 multiply_convert_fusion.3
  913.7 6.2 multiply_convert_fusion.3
  947.8 132.6 %while.58 = (s32[]{:T(128)}, f32[2048,3,64]{0,2,1:T(8,128)}, f32[2048,3,64]{0,2,1:T(8,128)}, bf16[4,512,3,64]{1,3,2,0:T(8,128)(2,1)}, s32[4]{0:T(128)S(1)}, /*in...) while((s32[]{:T(128)}, f32[2048,3,64]{0,2,1:T(8,128)}, ...), condition=%wide.region_20.20_spmd.clone, body=%wide.region_18.19_spmd.clone.sunk | while | flops 2063563264 | bytes 156690960 | solution.py:104
  964.2 6.2 multiply_convert_fusion.3
  996.6 6.2 multiply_convert_fusion.3
  1030.5 6.2 multiply_convert_fusion.3
  1064.4 6.2 multiply_convert_fusion.3
  1095.1 9.7 copy.67
  1111.7 7.0 convolution_convert_fusion
  1118.7 10.1 fusion.62
  1128.9 11.2 fusion.63
  1146.0 7.5 fusion.60
  1155.7 41.0 %psum.23 = f32[6,768]{1,0:T(8,128)} all-reduce(f32[6,768]{1,0:T(8,128)S(1)} %stack.39), channel_id=1, replica_groups=mesh['dp'=8,'tensor'=4] {'dp','tensor'}, use_global_device_ids=true, to_apply=%region_38.39 | all-reduce | flops 4608 | bytes 36864 | tf_op jit(solution)/shard_map/psum | solution.py:245
  1201.0 22.6 %all-reduce = (f32[2,192]{1,0:T(2,128)}, f32[768]{0:T(1024)}) all-reduce(f32[2,192]{1,0:T(2,128)S(1)} %pad_maximum_fusion, f32[768]{0:T(1024)S(1)} %copy-done.31), channel_id=1, replica_groups=mesh['dp'=8,'tensor'=4] {'dp'}, use_global_device_ids=true, to_apply=%region_26.27 | all-reduce | flops 1152 | bytes 9216 | tf_op jit(solution)/shard_map/psum | solution.py:244
  1227.0 24.6 %reduce-scatter.21.cloned.1.call-done = f32[96,768]{1,0:T(8,128)} async-done(((f32[768,768]{1,0:T(8,128)}), f32[96,768]{1,0:T(8,128)}) %reduce-scatter.21.cloned.1.call-update) | async-done | bytes 294928 | tf_op jit(solution)/shard_map/reduce_scatter | solution.py:241
  1251.6 72.4 %reduce-scatter.23.cloned.1.call-done = f32[96,768]{1,0:T(8,128)} async-done(((f32[768,768]{1,0:T(8,128)}), f32[96,768]{1,0:T(8,128)}) %reduce-scatter.23.cloned.1.call-update) | async-done | bytes 294928 | tf_op jit(solution)/shard_map/reduce_scatter | solution.py:242
  1324.1 65.9 %reduce-scatter.19.cloned.1.call-done = f32[96,192]{1,0:T(8,128)} async-done(((f32[768,192]{1,0:T(8,128)}), f32[96,192]{1,0:T(8,128)}) %reduce-scatter.19.cloned.1.call-update) | async-done | bytes 73744 | tf_op jit(solution)/shard_map/reduce_scatter | solution.py:240
  1390.0 71.9 %reduce-scatter.17.cloned.1.call-done = f32[96,3,192]{2,0,1:T(8,128)} async-done(((f32[768,3,192]{2,0,1:T(8,128)}), f32[96,3,192]{2,0,1:T(8,128)}) %reduce-scatter.17.cloned.1.call-update) | async-done | bytes 221200 | tf_op jit(solution)/shard_map/reduce_scatter | solution.py:239
  (444 shorter events, 346.7 us)
Async XLA Ops:
  8.0 41.6 %copy-start.24 = (bf16[96,192]{1,0:T(8,128)(2,1)S(1)}, bf16[96,192]{1,0:T(8,128)(2,1)}, u32[]{:S(2)}) copy-start(bf16[96,192]{1,0:T(8,128)(2,1)} %param.27) | copy-start | bytes 110596
  8.0 74.7 %copy-start.32 = (bf16[2,192]{1,0:T(2,128)(2,1)S(1)}, bf16[2,192]{1,0:T(2,128)(2,1)}, u32[]{:S(2)}) copy-start(bf16[2,192]{1,0:T(2,128)(2,1)} %param.26) | copy-start | bytes 2308
  8.0 74.7 %all-gather.7.cloned.1.call-start = ((), (), s32[]{:S(2)}) async-start(), calls=%async_computation.8 | async-start | bytes 7864320 | tf_op jit(solution)/shard_map/all_gather | solution.py:130
  8.8 411.7 %reduce-scatter.9.cloned.1.call-start = ((), (), s32[]{:S(2)}) async-start(), calls=%async_computation.9 | async-start | bytes 15728640 | tf_op jit(solution)/shard_map/reduce_scatter | solution.py:153
  49.6 33.2 %copy-start.20 = (bf16[768,3,192]{0,2,1:T(8,128)(2,1)}, bf16[768,3,192]{0,2,1:T(8,128)(2,1)S(1)}, u32[]{:S(2)}) copy-start(bf16[768,3,192]{0,2,1:T(8,128)(2,1)S(1)} %copy.56) | copy-start | bytes 2654212
  103.6 5.9 copy-start.23
  304.0 18.2 %copy-start.22 = (f32[2,4,3,512]{3,2,1,0:T(4,128)}, f32[2,4,3,512]{3,2,1,0:T(4,128)S(1)}, u32[]{:S(2)}) copy-start(f32[2,4,3,512]{3,2,1,0:T(4,128)S(1)} %get-tuple-element.826) | copy-start | bytes 147460
  304.0 11.7 copy-start.16
  322.2 104.0 %all-gather.11.cloned.1.call-start = ((), (), s32[]{:S(2)}) async-start(), calls=%async_computation.11 | async-start | bytes 1327104 | tf_op jit(solution)/shard_map/all_gather | solution.py:134
  322.8 149.1 %all-gather.9.cloned.1.call-start = ((), (), s32[]{:S(2)}) async-start(), calls=%async_computation.10 | async-start | bytes 7864320 | tf_op jit(solution)/shard_map/all_gather | solution.py:164
  425.6 90.0 %all-gather.13.cloned.1.call-start = ((), (), s32[]{:S(2)}) async-start(), calls=%async_computation.12 | async-start | bytes 1327104 | tf_op jit(solution)/shard_map/all_gather | solution.py:135
  426.2 155.4 %reduce-scatter.11.cloned.1.call-start = ((), (), s32[]{:S(2)}) async-start(), calls=%async_computation.13 | async-start | bytes 7864320 | tf_op jit(solution)/shard_map/reduce_scatter | solution.py:170
  524.7 112.9 %all-gather.15.cloned.1.call-start = ((), (), s32[]{:S(2)}) async-start(), calls=%async_computation.14 | async-start | bytes 7864320 | tf_op jit(solution)/shard_map/all_gather | solution.py:187
  591.3 133.6 %reduce-scatter.13.cloned.1.call-start = ((), (), s32[]{:S(2)}) async-start(), calls=%async_computation.15 | async-start | bytes 7864320 | tf_op jit(solution)/shard_map/reduce_scatter | solution.py:193
  637.6 19.0 %copy-start.40 = (bf16[768,768]{1,0:T(8,128)(2,1)S(1)}, bf16[768,768]{1,0:T(8,128)(2,1)}, u32[]{:S(2)}) copy-start(bf16[768,768]{1,0:T(8,128)(2,1)} %all-gather.11.cloned.1.call-done) | copy-start | bytes 3538948
  666.4 112.5 %all-gather.17.cloned.1.call-start = ((), (), s32[]{:S(2)}) async-start(), calls=%async_computation.16 | async-start | bytes 7864320 | tf_op jit(solution)/shard_map/all_gather | solution.py:204
  729.0 49.9 %copy-start.17 = (bf16[768,192]{1,0:T(8,128)(2,1)S(1)}, bf16[768,192]{1,0:T(8,128)(2,1)}, u32[]{:S(2)}) copy-start(bf16[768,192]{1,0:T(8,128)(2,1)} %all_gather.26) | copy-start | bytes 884740
  732.5 491.1 %reduce-scatter.15.cloned.1.call-start = ((), (), s32[]{:S(2)}) async-start(), calls=%async_computation.17 | async-start | bytes 7864320 | tf_op jit(solution)/shard_map/reduce_scatter | solution.py:232
  797.2 6.0 copy-start.2
  797.2 6.0 copy-start.5
  797.2 6.0 copy-start.7
  819.8 5.8 copy-start
  819.8 5.8 copy-start.6
  828.1 5.9 copy-start.2
  828.1 5.9 copy-start.5
  828.1 5.9 copy-start.7
  852.2 5.8 copy-start
  852.2 5.8 copy-start.6
  862.0 5.9 copy-start.2
  862.0 5.9 copy-start.5
  862.0 5.9 copy-start.7
  886.1 5.8 copy-start
  886.1 5.8 copy-start.6
  895.9 5.9 copy-start.2
  895.9 5.9 copy-start.5
  895.9 6.0 copy-start.7
  929.7 7.2 copy-start.4
  929.7 7.2 copy-start.18
  947.8 6.0 copy-start.2
  947.8 6.0 copy-start.5
  947.8 6.0 copy-start.7
  970.5 5.8 copy-start
  970.5 5.8 copy-start.6
  978.8 5.9 copy-start.2
  978.8 5.9 copy-start.5
  978.8 5.9 copy-start.7
  1002.8 5.8 copy-start
  1002.8 5.8 copy-start.6
  1012.7 5.9 copy-start.2
  1012.7 5.9 copy-start.5
  1012.7 5.9 copy-start.7
  1036.7 5.8 copy-start
  1036.7 5.8 copy-start.6
  1046.5 5.9 copy-start.2
  1046.5 5.9 copy-start.5
  1046.5 6.0 copy-start.7
  1080.4 7.1 copy-start.4
  1080.4 7.1 copy-start.18
  1118.7 133.0 %reduce-scatter.21.cloned.1.call-start = ((), (), s32[]{:S(2)}) async-start(), calls=%async_computation.20 | async-start | bytes 2654208 | tf_op jit(solution)/shard_map/reduce_scatter | solution.py:241
  1128.8 11.3 copy-start.13
  1128.8 195.2 %reduce-scatter.23.cloned.1.call-start = ((), (), s32[]{:S(2)}) async-start(), calls=%async_computation.21 | async-start | bytes 2654208 | tf_op jit(solution)/shard_map/reduce_scatter | solution.py:242
  1140.1 249.9 %reduce-scatter.19.cloned.1.call-start = ((), (), s32[]{:S(2)}) async-start(), calls=%async_computation.19 | async-start | bytes 884736 | tf_op jit(solution)/shard_map/reduce_scatter | solution.py:240
  1146.0 316.0 %reduce-scatter.17.cloned.1.call-start = ((), (), s32[]{:S(2)}) async-start(), calls=%async_computation.18 | async-start | bytes 2654208 | tf_op jit(solution)/shard_map/reduce_scatter | solution.py:239
  1200.4 23.3 %copy-start.10 = (f32[1024,768]{1,0:T(8,128)S(1)}, f32[1024,768]{1,0:T(8,128)}, u32[]{:S(2)}) copy-start(f32[1024,768]{1,0:T(8,128)} %get-tuple-element.384) | copy-start | bytes 9437188
  (50 other events, 135.7 us)
Sparse Core Ops, SparseCore 0:
  10.4 49.0 all-gather.6
  322.3 98.1 reduce-scatter.8
  666.5 58.3 reduce-scatter.12
Sparse Core Ops, SparseCore 1:
  324.9 40.5 all-gather.10
  425.7 46.2 all-gather.8
  474.0 41.5 all-gather.12
  524.8 56.7 reduce-scatter.10
  591.4 46.2 all-gather.14
  732.6 46.2 all-gather.16
  1118.8 58.9 reduce-scatter.14
  1182.0 69.5 reduce-scatter.20
  1256.0 68.0 reduce-scatter.22
  1328.3 61.6 reduce-scatter.18
  1393.9 68.0 reduce-scatter.16
where the time goes:
time: 1480 us; the launch traced here: 1470 us
  waiting for transfers between devices  596 us (40%)
  matrix products  424 us (29%)
  other arithmetic  146 us (10%)
  blocking collectives  135 us (9%)
  local copies, waits for them, and re-layouts  122 us (8%)
  loops' own time  27.8 us (2%)
  between operations  16.6 us (1%)
    reduce_scatter x1, waiting for transfers between devices, local(): lax.psum_scatter(times_transposed(context, out_full), 'tensor', scatter_d...  97.6 us
    reduce_scatter x1, waiting for transfers between devices, local(): lax.psum_scatter(down_grad, 'dp', scatter_dimension=0, tiled=True)  72.4 us
    reduce_scatter x1, waiting for transfers between devices, local(): lax.psum_scatter(qkv_g, 'dp', scatter_dimension=0, tiled=True)  71.9 us
    dot_general x16, matrix products, masked_scores(): jnp.einsum('qhd,khd->hqk', query_rows, key_seq, preferred_element_type=jn...  71.9 us
    reduce_scatter x1, waiting for transfers between devices, local(): lax.psum_scatter(out_weight_g, 'dp', scatter_dimension=0, tiled=True)  65.9 us
    dot_general x4, matrix products, matmul_plain(): return jnp.dot(left, right, preferred_element_type=jnp.float32)  64.8 us
    reduce_scatter x1, waiting for transfers between devices, local(): lax.psum_scatter(times_transposed(pre_grad, up_used).astype(jnp.bfloat16)...  58.5 us
    reduce_scatter x1, waiting for transfers between devices, local(): lax.psum_scatter(times_transposed(lax.slice_in_dim(act_low, 0, lax.axis_s...  56.1 us
  transfers between devices with their start and end apart: 14, of which 11 were waited for; matrix products, arithmetic and copies ran while one was open for 6% of the time, Pallas kernels for 0%

commit v1 on v0

--- a/solution.py
+++ b/solution.py
@@ -184,7 +184,13 @@
     )
     fed_low = grad_second.astype(jnp.bfloat16)
     down_bias_g = jnp.sum(fed_low.astype(jnp.float32), axis=0)
-    fed_rows = lax.all_gather(fed_low, "tensor", axis=0, tiled=True)
+    n_dev = lax.axis_size("tensor")
+    current, parts = (fed_low, [fed_low])
+    for _ in range(n_dev - 1):
+        current = lax.ppermute(current, "tensor", [(i, (i + 1) % n_dev) for i in range(n_dev)])
+        parts.insert(0, current)
+    line = jnp.concatenate(parts, axis=0)
+    fed_rows = jnp.roll(line, (lax.axis_index("tensor") + 1) * fed_low.shape[0], axis=0)
     act_grad = matmul_plain(fed_rows, down_used)
     pre_grad = gelu_back(act_grad)[0].astype(jnp.bfloat16)
     down_grad = over_rows(fed_rows, act_low)

time: 1480 us -> 1590 us (1.074)
  matrix products: 424 us -> 498 us
    ppermute x0 -> x3, waiting for transfers between devices: none -> 59.9 us  [local(): lax.ppermute(current, 'tensor', [(i, (i + 1) % n_dev) for i in range(n_de...]
    reduce_scatter x1, waiting for transfers between devices: 72.4 us -> 24.6 us  [local(): lax.psum_scatter(down_grad, 'dp', scatter_dimension=0, tiled=True)]
    reduce_scatter x1, waiting for transfers between devices: 24.6 us -> 72.4 us  [local(): lax.psum_scatter(up_grad, 'dp', scatter_dimension=0, tiled=True)]
    all_gather x1 -> x0, waiting for transfers between devices: 46.3 us -> none  [local(): fed_rows = lax.all_gather(fed_low, 'tensor', axis=0, tiled=True)]
    dot_general x16, matrix products: 71.9 us -> 108 us  [masked_scores(): jnp.einsum('qhd,khd->hqk', query_rows, key_seq, preferred_element_type=jn...]
    dot_general x8, matrix products: 46 us -> 80.2 us  [one_block(): jnp.einsum('hqk,qhd->khd', weights, grad_rows, preferred_element_type=jnp...]
    dot_general x8, matrix products: 46.5 us -> 16.2 us  [one_block(): jnp.einsum('hqk,khd->qhd', score_grad, key_seq, preferred_element_type=jn...]
    dot_general x8, matrix products: 28.8 us -> 46.3 us  [one_block(): jnp.einsum('hqk,qhd->khd', score_grad, query_rows, preferred_element_type...]
  transfers between devices with their start and end apart: 14 -> 16, of which waited for: 11 -> 13; matrix products, arithmetic and copies ran while one was open for 6% -> 5% of each run, Pallas kernels for 0% -> 0%
where the time goes in v1:
time: 1590 us; the launch traced here: 1570 us
  waiting for transfers between devices  610 us (38%)
  matrix products  498 us (31%)
  other arithmetic  153 us (10%)
  blocking collectives  136 us (9%)
  local copies, waits for them, and re-layouts  133 us (8%)
  loops' own time  27.8 us (2%)
  between operations  16.5 us (1%)
    dot_general x16, matrix products, masked_scores(): jnp.einsum('qhd,khd->hqk', query_rows, key_seq, preferred_element_type=jn...  108 us
    reduce_scatter x1, waiting for transfers between devices, local(): lax.psum_scatter(times_transposed(context, out_full), 'tensor', scatter_d...  97.6 us
    dot_general x8, matrix products, one_block(): jnp.einsum('hqk,qhd->khd', weights, grad_rows, preferred_element_type=jnp...  80.2 us
    reduce_scatter x1, waiting for transfers between devices, local(): lax.psum_scatter(up_grad, 'dp', scatter_dimension=0, tiled=True)  72.4 us
    reduce_scatter x1, waiting for transfers between devices, local(): lax.psum_scatter(qkv_g, 'dp', scatter_dimension=0, tiled=True)  72.2 us
    reduce_scatter x1, waiting for transfers between devices, local(): lax.psum_scatter(out_weight_g, 'dp', scatter_dimension=0, tiled=True)  65.7 us
    dot_general x4, matrix products, matmul_plain(): return jnp.dot(left, right, preferred_element_type=jnp.float32)  64.1 us
    dot_general x8, matrix products, one_block(): jnp.einsum('qhd,khd->hqk', grad_rows, value_seq, preferred_element_type=j...  63.3 us
  transfers between devices with their start and end apart: 16, of which 13 were waited for; matrix products, arithmetic and copies ran while one was open for 5% of the time, Pallas kernels for 0%

profile of v1, /device:TPU:0, one launch (start us, length us, event | category | flops | bytes accessed | tf_op | source)
XLA Modules:
  0.0 1574.7 jit_solution(4783129928843045149)
XLA Ops:
  9.9 38.8 %all_gather.22 = bf16[768,3,192]{2,1,0:T(4,128)(2,1)S(1)} all-gather(bf16[96,3,192]{2,1,0:T(4,128)(2,1)S(1)} %copy.55), channel_id=1, replica_groups=mesh['dp'=8,'tensor'=4] {'dp'}, dimensions={0}, use_global_device_ids=true | all-gather | bytes 995328 | tf_op jit(solution)/shard_map/all_gather | solution.py:132
  49.6 33.1 %all_gather.23 = bf16[768,192]{1,0:T(8,128)(2,1)} all-gather(bf16[96,192]{1,0:T(8,128)(2,1)S(1)} %copy-done.29), channel_id=1, replica_groups=mesh['dp'=8,'tensor'=4] {'dp'}, dimensions={0}, use_global_device_ids=true | all-gather | bytes 331776 | tf_op jit(solution)/shard_map/all_gather | solution.py:133
  109.4 194.2 %while.54 = (s32[]{:T(128)}, bf16[2,2048,3,64]{3,2,1,0:T(4,128)(2,1)}, f32[2,4,3,512]{3,2,1,0:T(4,128)S(1)}, bf16[2,2048,3,64]{1,3,2,0:T(8,128)(2,1)}, s32[2,204...) while((s32[]{:T(128)}, ...), condition=%wide.region_5.6_spmd, body=%wide.region_0.5_spmd.sunk | while | flops 844102144 | bytes 53437376 | solution.py:151
  113.1 90.3 %while.57 = (s32[]{:T(128)}, bf16[4,512,3,64]{1,3,2,0:T(8,128)(2,1)S(1)}, f32[4,3,512]{2,1,0:T(4,128)S(1)}, s32[4]{0:T(128)S(1)}, s32[2048]{0:T(1024)S(1)}, /*in...) while((s32[]{:T(128)}, ...), condition=%wide.region_4.4_spmd, body=%wide.region_1.3_spmd.sunk | while | flops 844102144 | bytes 44179644 | solution.py:67
  115.1 7.1 fusion.133
  122.2 6.8 fusion.134
  137.6 7.1 fusion.133
  144.7 6.8 fusion.134
  160.2 7.1 fusion.133
  167.3 6.8 fusion.134
  182.8 7.1 fusion.133
  189.9 6.8 fusion.134
  210.2 90.3 %while.57 = (s32[]{:T(128)}, bf16[4,512,3,64]{1,3,2,0:T(8,128)(2,1)S(1)}, f32[4,3,512]{2,1,0:T(4,128)S(1)}, s32[4]{0:T(128)S(1)}, s32[2048]{0:T(1024)S(1)}, /*in...) while((s32[]{:T(128)}, ...), condition=%wide.region_4.4_spmd, body=%wide.region_1.3_spmd.sunk | while | flops 844102144 | bytes 44179644 | solution.py:67
  212.2 7.1 fusion.133
  219.2 6.8 fusion.134
  234.7 7.1 fusion.133
  241.8 6.8 fusion.134
  257.3 7.1 fusion.133
  264.4 6.8 fusion.134
  279.9 7.1 fusion.133
  303.6 10.0 copy.60
  322.6 97.6 %reduce-scatter.9.cloned.1.call-done = f32[1024,768]{1,0:T(8,128)} async-done(((f32[4096,768]{1,0:T(8,128)}), f32[1024,768]{1,0:T(8,128)}) %reduce-scatter.9.cloned.1.call-update) | async-done | bytes 3145744 | tf_op jit(solution)/shard_map/reduce_scatter | solution.py:153
  425.9 45.7 %all-gather.8.cloned.1.call-done = bf16[4096,768]{1,0:T(8,128)(2,1)} async-done(((bf16[1024,768]{1,0:T(8,128)(2,1)}), bf16[4096,768]{1,0:T(8,128)(2,1)}) %all-gather.8.cloned.1.call-update) | async-done | bytes 6291472 | tf_op jit(solution)/shard_map/all_gather | solution.py:164
  471.6 34.9 %multiply_convert_fusion.1 = (bf16[4096,768]{1,0:T(8,128)(2,1)}, f32[4096,768]{1,0:T(8,128)}, f32[4096,768]{1,0:T(8,128)}) fusion(f32[768]{0:T(1024)S(1)} %convert_element_type.114, bf16[4096,768]{1,0:T(8,128)(2,1)} %all-gather.8.cloned.1.call-done, bf16[768,768]{1,0:T(8,128)(2,1)} %all-gather.10.cloned.1.call-done), kind=kOutput, calls=%fused_computation.62 | convolution fusion | flops 5039456256 | bytes 38931456 | tf_op jit(solution)/shard_map/dot_general | solution.py:13
  506.4 8.6 all-gather.12.cloned.1.call-done
  515.0 9.2 convolution_convert_fusion.2
  525.0 56.1 %reduce-scatter.11.cloned.1.call-done = bf16[1024,768]{1,0:T(8,128)(2,1)} async-done(((bf16[4096,768]{1,0:T(8,128)(2,1)}), bf16[1024,768]{1,0:T(8,128)(2,1)}) %reduce-scatter.11.cloned.1.call-update) | async-done | bytes 1572880 | tf_op jit(solution)/shard_map/reduce_scatter | solution.py:170
  591.7 19.8 %collective-permute-done = bf16[1024,768]{1,0:T(8,128)(2,1)S(1)} collective-permute-done((bf16[1024,768]{1,0:T(8,128)(2,1)S(1)}, bf16[1024,768]{1,0:T(8,128)(2,1)S(1)}, u32[]{:S(2)}, u32[]{:S(2)}) %collective-permute-start) | collective-permute-done | bytes 1572896 | tf_op jit(solution)/shard_map/ppermute | solution.py:190
  612.6 19.9 %collective-permute-done.1 = bf16[1024,768]{1,0:T(8,128)(2,1)} collective-permute-done((bf16[1024,768]{1,0:T(8,128)(2,1)S(1)}, bf16[1024,768]{1,0:T(8,128)(2,1)}, u32[]{:S(2)}, u32[]{:S(2)}) %collective-permute-start.1) | collective-permute-done | bytes 1572896 | tf_op jit(solution)/shard_map/ppermute | solution.py:190
  632.6 20.1 %collective-permute-done.2 = bf16[1024,768]{1,0:T(8,128)(2,1)} collective-permute-done((bf16[1024,768]{1,0:T(8,128)(2,1)}, bf16[1024,768]{1,0:T(8,128)(2,1)}, u32[]{:S(2)}, u32[]{:S(2)}) %collective-permute-start.2) | collective-permute-done | bytes 1572896 | tf_op jit(solution)/shard_map/ppermute | solution.py:190
  663.9 18.3 %convert_reduce_fusion = (f32[768]{0:T(1024)}, bf16[4096,768]{1,0:T(8,128)(2,1)}) fusion(f32[4096,768]{1,0:T(8,128)} %get-tuple-element.388, bf16[768,768]{1,0:T(8,128)(2,1)S(1)} %copy-done.46, bf16[8192,768]{1,0:T(8,128)(2,1)} %copy-done.28, s32[]{:T(128)S(6)} %select_n.33, f32[4096,768]{1,0:T(8,128)} %get-tuple-element.404, f32[768]{0:T(1024)S(1)} %convert_element_type.114), kind=kOutput, calls=%fused_computation.60 | convolution fusion | flops 4885314560 | bytes 38934532 | tf_op jit(solution)/shard_map/dot_general | solution.py:13
  682.1 9.7 convolution_convert_fusion.1
  691.9 58.3 %reduce-scatter.13.cloned.1.call-done = bf16[1024,768]{1,0:T(8,128)(2,1)} async-done(((bf16[4096,768]{1,0:T(8,128)(2,1)}), bf16[1024,768]{1,0:T(8,128)(2,1)}) %reduce-scatter.13.cloned.1.call-update) | async-done | bytes 1572880 | tf_op jit(solution)/shard_map/reduce_scatter | solution.py:199
  757.9 46.5 %all-gather.14.cloned.1.call-done = bf16[4096,768]{1,0:T(8,128)(2,1)} async-done(((bf16[1024,768]{1,0:T(8,128)(2,1)}), bf16[4096,768]{1,0:T(8,128)(2,1)}) %all-gather.14.cloned.1.call-update) | async-done | bytes 6291472 | tf_op jit(solution)/shard_map/all_gather | solution.py:210
  815.2 383.9 %while.56 = (s32[]{:T(128)}, bf16[2,2048,3,64]{3,2,1,0:T(4,128)(2,1)}, bf16[2,2048,3,64]{1,3,2,0:T(8,128)(2,1)}, bf16[2,2048,3,64]{1,3,2,0:T(8,128)(2,1)}, bf16[...) while((s32[]{:T(128)}, ...), condition=%wide.region_21.22_spmd, body=%wide.region_17.21_spmd.sunk | while | flops 2063563264 | bytes 214689712 | solution.py:219
  823.5 177.1 %while.58 = (s32[]{:T(128)}, f32[2048,3,64]{0,2,1:T(8,128)}, f32[2048,3,64]{0,2,1:T(8,128)}, bf16[4,512,3,64]{1,3,2,0:T(8,128)(2,1)}, s32[4]{0:T(128)S(1)}, /*in...) while((s32[]{:T(128)}, f32[2048,3,64]{0,2,1:T(8,128)}, ...), condition=%wide.region_20.20_spmd.clone, body=%wide.region_18.19_spmd.clone.sunk | while | flops 2063563264 | bytes 194437712 | solution.py:104
  835.0 7.9 multiply_reduce_fusion.7
  857.5 9.7 fusion.129
  878.6 7.9 multiply_reduce_fusion.7
  901.5 10.1 fusion.129
  923.1 7.9 multiply_reduce_fusion.7
  946.0 10.1 fusion.129
  967.5 7.9 multiply_reduce_fusion.7
  990.5 10.1 fusion.129
  1015.3 177.1 %while.58 = (s32[]{:T(128)}, f32[2048,3,64]{0,2,1:T(8,128)}, f32[2048,3,64]{0,2,1:T(8,128)}, bf16[4,512,3,64]{1,3,2,0:T(8,128)(2,1)}, s32[4]{0:T(128)S(1)}, /*in...) while((s32[]{:T(128)}, f32[2048,3,64]{0,2,1:T(8,128)}, ...), condition=%wide.region_20.20_spmd.clone, body=%wide.region_18.19_spmd.clone.sunk | while | flops 2063563264 | bytes 194437712 | solution.py:104
  1026.7 7.9 multiply_reduce_fusion.7
  1049.2 9.7 fusion.129
  1070.4 7.9 multiply_reduce_fusion.7
  1093.3 10.1 fusion.129
  1114.8 7.9 multiply_reduce_fusion.7
  1137.8 10.1 fusion.129
  1159.3 7.9 multiply_reduce_fusion.7
  1182.3 10.1 fusion.129
  1199.1 9.8 copy.67
  1216.7 7.1 convolution_convert_fusion
  1223.8 10.1 fusion.42
  1234.0 11.2 fusion.70
  1251.2 7.5 fusion.68
  1260.9 41.0 %psum.23 = f32[6,768]{1,0:T(8,128)} all-reduce(f32[6,768]{1,0:T(8,128)S(1)} %stack.39), channel_id=1, replica_groups=mesh['dp'=8,'tensor'=4] {'dp','tensor'}, use_global_device_ids=true, to_apply=%region_38.39 | all-reduce | flops 4608 | bytes 36864 | tf_op jit(solution)/shard_map/psum | solution.py:251
  1306.3 22.5 %all-reduce = (f32[2,192]{1,0:T(2,128)}, f32[768]{0:T(1024)}) all-reduce(f32[2,192]{1,0:T(2,128)S(1)} %pad_maximum_fusion, f32[768]{0:T(1024)S(1)} %copy-done.36), channel_id=1, replica_groups=mesh['dp'=8,'tensor'=4] {'dp'}, use_global_device_ids=true, to_apply=%region_26.27 | all-reduce | flops 1152 | bytes 9216 | tf_op jit(solution)/shard_map/psum | solution.py:250
  1332.2 24.6 %reduce-scatter.23.cloned.1.call-done = f32[96,768]{1,0:T(8,128)} async-done(((f32[768,768]{1,0:T(8,128)}), f32[96,768]{1,0:T(8,128)}) %reduce-scatter.23.cloned.1.call-update) | async-done | bytes 294928 | tf_op jit(solution)/shard_map/reduce_scatter | solution.py:248
  1356.8 72.4 %reduce-scatter.21.cloned.1.call-done = f32[96,768]{1,0:T(8,128)} async-done(((f32[768,768]{1,0:T(8,128)}), f32[96,768]{1,0:T(8,128)}) %reduce-scatter.21.cloned.1.call-update) | async-done | bytes 294928 | tf_op jit(solution)/shard_map/reduce_scatter | solution.py:247
  1429.2 65.7 %reduce-scatter.19.cloned.1.call-done = f32[96,192]{1,0:T(8,128)} async-done(((f32[768,192]{1,0:T(8,128)}), f32[96,192]{1,0:T(8,128)}) %reduce-scatter.19.cloned.1.call-update) | async-done | bytes 73744 | tf_op jit(solution)/shard_map/reduce_scatter | solution.py:246
  1494.9 72.2 %reduce-scatter.17.cloned.1.call-done = f32[96,3,192]{2,0,1:T(8,128)} async-done(((f32[768,3,192]{2,0,1:T(8,128)}), f32[96,3,192]{2,0,1:T(8,128)}) %reduce-scatter.17.cloned.1.call-update) | async-done | bytes 221200 | tf_op jit(solution)/shard_map/reduce_scatter | solution.py:245
  (519 shorter events, 412.1 us)
Async XLA Ops:
  8.0 41.6 %copy-start.29 = (bf16[96,192]{1,0:T(8,128)(2,1)S(1)}, bf16[96,192]{1,0:T(8,128)(2,1)}, u32[]{:S(2)}) copy-start(bf16[96,192]{1,0:T(8,128)(2,1)} %param.27) | copy-start | bytes 110596
  8.0 74.7 %copy-start.37 = (bf16[2,192]{1,0:T(2,128)(2,1)S(1)}, bf16[2,192]{1,0:T(2,128)(2,1)}, u32[]{:S(2)}) copy-start(bf16[2,192]{1,0:T(2,128)(2,1)} %param.26) | copy-start | bytes 2308
  8.0 74.7 %all-gather.6.cloned.1.call-start = ((), (), s32[]{:S(2)}) async-start(), calls=%async_computation.8 | async-start | bytes 7864320 | tf_op jit(solution)/shard_map/all_gather | solution.py:130
  8.8 411.4 %reduce-scatter.9.cloned.1.call-start = ((), (), s32[]{:S(2)}) async-start(), calls=%async_computation.9 | async-start | bytes 15728640 | tf_op jit(solution)/shard_map/reduce_scatter | solution.py:153
  49.6 39.2 %copy-start.24 = (bf16[768,3,192]{0,2,1:T(8,128)(2,1)}, bf16[768,3,192]{0,2,1:T(8,128)(2,1)S(1)}, u32[]{:S(2)}) copy-start(bf16[768,3,192]{0,2,1:T(8,128)(2,1)S(1)} %copy.56) | copy-start | bytes 2654212
  303.6 18.2 %copy-start.26 = (f32[2,4,3,512]{3,2,1,0:T(4,128)}, f32[2,4,3,512]{3,2,1,0:T(4,128)S(1)}, u32[]{:S(2)}) copy-start(f32[2,4,3,512]{3,2,1,0:T(4,128)S(1)} %get-tuple-element.826) | copy-start | bytes 147460
  303.6 11.8 copy-start.20
  321.9 104.0 %all-gather.10.cloned.1.call-start = ((), (), s32[]{:S(2)}) async-start(), calls=%async_computation.11 | async-start | bytes 1327104 | tf_op jit(solution)/shard_map/all_gather | solution.py:134
  322.5 149.1 %all-gather.8.cloned.1.call-start = ((), (), s32[]{:S(2)}) async-start(), calls=%async_computation.10 | async-start | bytes 7864320 | tf_op jit(solution)/shard_map/all_gather | solution.py:164
  425.2 89.8 %all-gather.12.cloned.1.call-start = ((), (), s32[]{:S(2)}) async-start(), calls=%async_computation.12 | async-start | bytes 1327104 | tf_op jit(solution)/shard_map/all_gather | solution.py:135
  425.8 155.3 %reduce-scatter.11.cloned.1.call-start = ((), (), s32[]{:S(2)}) async-start(), calls=%async_computation.13 | async-start | bytes 7864320 | tf_op jit(solution)/shard_map/reduce_scatter | solution.py:170
  524.3 226.0 %reduce-scatter.13.cloned.1.call-start = ((), (), s32[]{:S(2)}) async-start(), calls=%async_computation.14 | async-start | bytes 7864320 | tf_op jit(solution)/shard_map/reduce_scatter | solution.py:199
  591.6 19.8 %collective-permute-start = (bf16[1024,768]{1,0:T(8,128)(2,1)S(1)}, bf16[1024,768]{1,0:T(8,128)(2,1)S(1)}, u32[]{:S(2)}, u32[]{:S(2)}) collective-permute-start(bf16[1024,768]{1,0:T(8,128)(2,1)S(1)} %get-tuple-element.380), channel_id=1, source_target_pairs={{0,1},{1,2},{2,3},{3,0},{4,5},{5,6},{6,7},{7,4},{8,9},{9,10},{10,1... | collective-permute-start | bytes 4718600 | tf_op jit(solution)/shard_map/ppermute | solution.py:190
  612.6 19.9 %collective-permute-start.1 = (bf16[1024,768]{1,0:T(8,128)(2,1)S(1)}, bf16[1024,768]{1,0:T(8,128)(2,1)}, u32[]{:S(2)}, u32[]{:S(2)}) collective-permute-start(bf16[1024,768]{1,0:T(8,128)(2,1)S(1)} %collective-permute-done), channel_id=1, source_target_pairs={{0,1},{1,2},{2,3},{3,0},{4,5},{5,6},{6,7},{7,4},{8,9},{9,10},{10,1... | collective-permute-start | bytes 4718600 | tf_op jit(solution)/shard_map/ppermute | solution.py:190
  632.6 20.2 %collective-permute-start.2 = (bf16[1024,768]{1,0:T(8,128)(2,1)}, bf16[1024,768]{1,0:T(8,128)(2,1)}, u32[]{:S(2)}, u32[]{:S(2)}) collective-permute-start(bf16[1024,768]{1,0:T(8,128)(2,1)} %collective-permute-done.1), channel_id=1, source_target_pairs={{0,1},{1,2},{2,3},{3,0},{4,5},{5,6},{6,7},{7,4},{8,9},{9,10},{10,1... | collective-permute-start | bytes 4718600 | tf_op jit(solution)/shard_map/ppermute | solution.py:190
  632.6 23.2 %copy-start.17 = (bf16[1024,768]{1,0:T(8,128)(2,1)S(1)}, bf16[1024,768]{1,0:T(8,128)(2,1)}, u32[]{:S(2)}) copy-start(bf16[1024,768]{1,0:T(8,128)(2,1)} %copy-done.16) | copy-start | bytes 4718596
  632.6 23.3 %copy-start.11 = (bf16[1024,768]{1,0:T(8,128)(2,1)S(1)}, bf16[1024,768]{1,0:T(8,128)(2,1)}, u32[]{:S(2)}) copy-start(bf16[1024,768]{1,0:T(8,128)(2,1)} %copy-done.10) | copy-start | bytes 4718596
  663.9 18.3 %copy-start.45 = (bf16[768,768]{1,0:T(8,128)(2,1)S(1)}, bf16[768,768]{1,0:T(8,128)(2,1)}, u32[]{:S(2)}) copy-start(bf16[768,768]{1,0:T(8,128)(2,1)} %all-gather.10.cloned.1.call-done) | copy-start | bytes 3538948
  691.9 112.5 %all-gather.14.cloned.1.call-start = ((), (), s32[]{:S(2)}) async-start(), calls=%async_computation.15 | async-start | bytes 7864320 | tf_op jit(solution)/shard_map/all_gather | solution.py:210
  754.3 50.1 %copy-start.21 = (bf16[768,192]{1,0:T(8,128)(2,1)S(1)}, bf16[768,192]{1,0:T(8,128)(2,1)}, u32[]{:S(2)}) copy-start(bf16[768,192]{1,0:T(8,128)(2,1)} %all_gather.23) | copy-start | bytes 884740
  757.9 570.9 %reduce-scatter.15.cloned.1.call-start = ((), (), s32[]{:S(2)}) async-start(), calls=%async_computation.16 | async-start | bytes 7864320 | tf_op jit(solution)/shard_map/reduce_scatter | solution.py:238
  834.9 8.0 slice-start
  834.9 8.0 slice-start.1
  834.9 8.8 slice-start.2
  857.4 9.7 copy-start.8
  857.4 9.7 copy-start.5
  878.6 8.0 slice-start
  878.6 8.0 slice-start.1
  878.6 8.8 slice-start.2
  901.5 10.2 copy-start.8
  901.5 10.1 copy-start.5
  923.0 8.0 slice-start
  923.0 8.0 slice-start.1
  923.1 8.8 slice-start.2
  946.0 10.2 copy-start.8
  946.0 10.1 copy-start.5
  967.5 8.8 slice-start.2
  990.5 10.2 copy-start.8
  990.5 10.1 copy-start.5
  1026.7 8.0 slice-start
  1026.7 8.0 slice-start.1
  1026.7 8.8 slice-start.2
  1049.2 9.7 copy-start.8
  1049.2 9.7 copy-start.5
  1070.3 8.0 slice-start
  1070.3 8.0 slice-start.1
  1070.3 8.8 slice-start.2
  1093.3 10.2 copy-start.8
  1093.3 10.1 copy-start.5
  1114.8 8.0 slice-start
  1114.8 8.0 slice-start.1
  1114.8 8.8 slice-start.2
  1137.7 10.2 copy-start.8
  1137.7 10.1 copy-start.5
  1159.3 8.8 slice-start.2
  1182.2 10.2 copy-start.8
  1182.2 10.1 copy-start.5
  1199.1 10.6 copy-start.22
  1223.7 133.0 %reduce-scatter.23.cloned.1.call-start = ((), (), s32[]{:S(2)}) async-start(), calls=%async_computation.20 | async-start | bytes 2654208 | tf_op jit(solution)/shard_map/reduce_scatter | solution.py:248
  1233.9 11.3 copy-start.15
  1233.9 195.3 %reduce-scatter.21.cloned.1.call-start = ((), (), s32[]{:S(2)}) async-start(), calls=%async_computation.19 | async-start | bytes 2654208 | tf_op jit(solution)/shard_map/reduce_scatter | solution.py:247
  1245.2 249.7 %reduce-scatter.19.cloned.1.call-start = ((), (), s32[]{:S(2)}) async-start(), calls=%async_computation.18 | async-start | bytes 884736 | tf_op jit(solution)/shard_map/reduce_scatter | solution.py:246
  1251.2 316.0 %reduce-scatter.17.cloned.1.call-start = ((), (), s32[]{:S(2)}) async-start(), calls=%async_computation.17 | async-start | bytes 2654208 | tf_op jit(solution)/shard_map/reduce_scatter | solution.py:245
  1305.6 23.2 %copy-start.12 = (f32[1024,768]{1,0:T(8,128)S(1)}, f32[1024,768]{1,0:T(8,128)}, u32[]{:S(2)}) copy-start(f32[1024,768]{1,0:T(8,128)} %get-tuple-element.384) | copy-start | bytes 9437188
  (80 other events, 376.8 us)
Sparse Core Ops, SparseCore 0:
  10.4 49.0 all-gather.5
  322.0 98.1 reduce-scatter.8
  758.0 46.3 all-gather.13
Sparse Core Ops, SparseCore 1:
  324.5 40.6 all-gather.9
  425.3 46.2 all-gather.7
  473.6 41.3 all-gather.11
  524.4 56.7 reduce-scatter.10
  692.0 58.2 reduce-scatter.12
  1223.8 58.9 reduce-scatter.14
  1287.1 69.6 reduce-scatter.22
  1361.1 68.0 reduce-scatter.20
  1433.3 61.6 reduce-scatter.18
  1499.0 68.1 reduce-scatter.16
